TPU v7x, 32 devices: a whole 2x2x4 slice. The times are simulated.
32 devices in a mesh: cp: 8 (over z, y), grp: 4 (over x, core).
Axes of the slice: x: 2, y: 2, z: 4, core: 2. Of those that a mesh axis runs over, the one named last changes fastest.
Arguments:
- queries: bfloat16 [4096, 4096], P('cp', 'grp'), parts along dimension 1, may hold values from -22.5 to 22.5
- keys: bfloat16 [4096, 512], P('cp', 'grp'), parts along dimension 1, may hold values from -7.5 to 7.5
- values: bfloat16 [4096, 512], P('cp', 'grp'), parts along dimension 1, may hold values from -6 to 6
- grad_out: bfloat16 [4096, 4096], P('cp', 'grp'), parts along dimension 1, may hold values from -6 to 6
- segments: int32 [4096], P('cp'), may hold values from 0 to 15, never falling along the last dimension, each value on 1 to 1025 neighbouring positions
Outputs:
- attended: bfloat16 [4096, 4096], P('cp', 'grp'), parts along dimension 1
- grad_queries: bfloat16 [4096, 4096], P('cp', 'grp'), parts along dimension 1
- grad_keys: bfloat16 [4096, 512], P('cp', 'grp'), parts along dimension 1
- grad_values: bfloat16 [4096, 512], P('cp', 'grp'), parts along dimension 1
There are 4 independent parts, one for each index of `grp`. A program takes and returns all parts, laid end to end along the dimension named above; an argument that names none is the same for every part. Nothing has to cross between parts.
All inputs are finite; a program needn't handle non-finite values.
Results may differ from a plain program's by a relative error of at most 0.028.
Values may be sent and summed in bfloat16 or wider, within the bound.
A program may use at most 128 MiB of HBM per device.

v0:
```python
import math

import jax
import jax.numpy as jnp
from jax import lax
from jax.sharding import PartitionSpec as P

REACH = 2


NEG = -1e30


def shifted(value, axis, steps):
    count = lax.axis_size(axis)
    first, last = (max(0, -steps), min(count, count - steps))
    return lax.ppermute(value, axis, [(source, source + steps) for source in range(first, last)])


def for_sending(x):

    def short(part):
        return part.astype(jnp.bfloat16) if part.dtype == jnp.float32 else part

    return jax.tree.map(short, x)


def pair_scores(query_tile, key_tile, query_pos, key_pos, seg_query, seg_key, valid, scale):
    scores = (
        jnp.einsum("qhd,kd->hqk", query_tile, key_tile, preferred_element_type=jnp.float32) * scale
    )
    allowed = (
        (seg_query[:, None] == seg_key[None, :]) & (key_pos[None, :] <= query_pos[:, None]) & valid
    )
    return (scores, allowed)


def pair_stats(scores, allowed):
    peak = jnp.max(jnp.where(allowed[None], scores, NEG), axis=-1)
    total = jnp.sum(jnp.where(allowed[None], jnp.exp(scores - peak[..., None]), 0.0), axis=-1)
    return (peak, total)


def merge_stats(first, second):
    peak = jnp.maximum(first[0], second[0])
    total = first[1] * jnp.exp(first[0] - peak) + second[1] * jnp.exp(second[0] - peak)
    return (peak, total)


def pair_output(scores, allowed, lse, value_tile):
    probs = jnp.where(allowed[None], jnp.exp(scores - lse[..., None]), 0.0)
    probs_low = probs.astype(jnp.bfloat16)
    term = jnp.einsum("hqk,kd->qhd", probs_low, value_tile, preferred_element_type=jnp.float32)
    return (term, probs, probs_low)


def pair_backward(probs, probs_low, grad_tile, delta, query_tile, key_tile, value_tile, scale):
    dprobs = jnp.einsum("qhd,kd->hqk", grad_tile, value_tile, preferred_element_type=jnp.float32)
    dscores = (probs * (dprobs - delta[..., None])).astype(jnp.bfloat16)
    grad_q = (
        jnp.einsum("hqk,kd->qhd", dscores, key_tile, preferred_element_type=jnp.float32) * scale
    )
    grad_k = (
        jnp.einsum("hqk,qhd->kd", dscores, query_tile, preferred_element_type=jnp.float32) * scale
    )
    grad_v = jnp.einsum("hqk,qhd->kd", probs_low, grad_tile, preferred_element_type=jnp.float32)
    return (grad_q, grad_k, grad_v)


def on_device(queries, keys, values, grad_out, segments):
    rows, width = queries.shape
    head_size = keys.shape[1]
    heads = width // head_size
    scale = 1.0 / math.sqrt(head_size)
    me = lax.axis_index("cp")
    line = jnp.arange(rows, dtype=jnp.int32)
    own_pos = me * rows + line
    query_tile = queries.reshape(rows, heads, head_size)
    grad_tile = grad_out.reshape(rows, heads, head_size)
    windows = [(keys, values, segments)]
    for dist in range(1, REACH + 1):
        windows.append(shifted((keys, values, segments), "cp", dist))
    scored = []
    for dist in range(REACH + 1):
        key_pos = (me - dist) * rows + line
        scored.append(
            pair_scores(
                query_tile,
                windows[dist][0],
                own_pos,
                key_pos,
                segments,
                windows[dist][2],
                me - dist >= 0,
                scale,
            )
        )
    stats = pair_stats(scored[0][0], scored[0][1])
    for dist in range(1, REACH + 1):
        stats = merge_stats(stats, pair_stats(scored[dist][0], scored[dist][1]))
    lse = stats[0] + jnp.log(stats[1])
    out_sum = jnp.zeros((rows, heads, head_size), jnp.float32)
    kept = []
    for dist in range(REACH + 1):
        term, probs, probs_low = pair_output(
            scored[dist][0], scored[dist][1], lse, windows[dist][1]
        )
        out_sum = out_sum + term
        kept.append((probs, probs_low))
    attended = out_sum.astype(jnp.bfloat16)
    delta = jnp.sum(grad_tile.astype(jnp.float32) * attended.astype(jnp.float32), axis=-1).T
    grad_q_sum = jnp.zeros((rows, heads, head_size), jnp.float32)
    grad_k_sum = jnp.zeros((rows, head_size), jnp.float32)
    grad_v_sum = jnp.zeros((rows, head_size), jnp.float32)
    remote = []
    for dist in range(REACH + 1):
        grad_q, grad_k, grad_v = pair_backward(
            kept[dist][0],
            kept[dist][1],
            grad_tile,
            delta,
            query_tile,
            windows[dist][0],
            windows[dist][1],
            scale,
        )
        grad_q_sum = grad_q_sum + grad_q
        if dist == 0:
            grad_k_sum = grad_k
            grad_v_sum = grad_v
        else:
            remote.append((grad_k, grad_v))
    for dist in range(1, REACH + 1):
        back_k, back_v = shifted(for_sending(remote[dist - 1]), "cp", -dist)
        grad_k_sum = grad_k_sum + back_k
        grad_v_sum = grad_v_sum + back_v
    return (
        attended.reshape(rows, width),
        grad_q_sum.astype(jnp.bfloat16).reshape(rows, width),
        grad_k_sum.astype(jnp.bfloat16),
        grad_v_sum.astype(jnp.bfloat16),
    )


def solution(mesh):
    placed = (P("cp", "grp"), P("cp", "grp"), P("cp", "grp"), P("cp", "grp"), P("cp"))
    return jax.shard_map(
        on_device,
        mesh=mesh,
        in_specs=placed,
        out_specs=(P("cp", "grp"), P("cp", "grp"), P("cp", "grp"), P("cp", "grp")),
        check_vma=False,
    )
```

profile of v0, /device:TPU:26, one launch (start us, length us, event | category | flops | bytes accessed | tf_op | source)
XLA Modules:
  0.0 90.5 jit_solution(8365786845835908620)
XLA Ops:
  2.1 3.4 %collective-permute-start = (s32[512]{0:T(512)}, s32[512]{0:T(512)S(1)}, u32[]{:S(2)}, u32[]{:S(2)}) collective-permute-start(s32[512]{0:T(512)} %param.9), channel_id=1, source_target_pairs={{0,4},{4,8},{8,12},{12,16},{16,20},{20,24},{24,28},{1,5},{5,9},{9,... | collective-permute-start | bytes 6152 | tf_op jit(solution)/shard_map/ppermute | solution.py:17
  7.8 1.9 %collective-permute-start.4 = (bf16[512,128]{0,1:T(8,128)(2,1)S(1)}, bf16[512,128]{0,1:T(8,128)(2,1)S(1)}, u32[]{:S(2)}, u32[]{:S(2)}) collective-permute-start(bf16[512,128]{0,1:T(8,128)(2,1)S(1)} %copy.14), channel_id=1, source_target_pairs={{0,4},{4,8},{8,12},{12,16},{16,20},{20,24},{24,28},{1,5},{5,9},{9,... | collective-permute-start | bytes 393224 | tf_op jit(solution)/shard_map/ppermute | solution.py:17
  9.8 1.9 %collective-permute-start.1 = (bf16[512,128]{1,0:T(8,128)(2,1)}, bf16[512,128]{1,0:T(8,128)(2,1)S(1)}, u32[]{:S(2)}, u32[]{:S(2)}) collective-permute-start(bf16[512,128]{1,0:T(8,128)(2,1)} %param.6), channel_id=1, source_target_pairs={{0,4},{4,8},{8,12},{12,16},{16,20},{20,24},{24,28},{1,5},{5,9},{9,... | collective-permute-start | bytes 393224 | tf_op jit(solution)/shard_map/ppermute | solution.py:17
  14.6 1.8 %and_and_fusion.2 = (pred[512,512]{0,1:T(8,128)(4,1)S(1)}, pred[512,512]{0,1:T(8,128)(4,1)S(1)}, pred[512,512]{0,1:T(8,128)(4,1)S(1)}) fusion(s32[512]{0:T(512)S(1)} %iota_add_fusion.2, s32[512]{0:T(512)} %param.9, pred[]{:T(512)S(6)} %ge.9, pred[]{:T(512)S(6)} %ge.11, s32[512]{0:T(512)S(1)} %get-tuple-element.19, s32[512]{0:T(512)S(1)} %collective-permute-done.2, ...), kind=kLoop, calls=%fused_computation.66 | loop fusion | flops 3145728 | bytes 798723 | tf_op jit(solution)/shard_map/and | solution.py:33
  16.4 2.6 %fusion.18 = (f32[8,512]{1,0:T(8,128)S(1)}, f32[512,512,8]{1,0,2:T(8,128)S(1)}) fusion(pred[512,512]{0,1:T(8,128)(4,1)S(1)} %get-tuple-element.8, bf16[512,128]{1,0:T(8,128)(2,1)} %param.6, bf16[512,1024]{1,0:T(8,128)(2,1)S(1)} %copy-done), kind=kOutput, calls=%fused_computation.30 | convolution fusion | flops 543158272 | bytes 9846784 | tf_op jit(solution)/shard_map/qhd,kd->hqk/dot_general | solution.py:30
  21.8 1.8 %fusion.6 = (f32[8,512]{1,0:T(8,128)S(1)}, f32[512,512,8]{1,0,2:T(8,128)S(1)}) fusion(pred[512,512]{0,1:T(8,128)(4,1)S(1)} %get-tuple-element.9, bf16[512,128]{1,0:T(8,128)(2,1)S(1)} %collective-permute-done.3, bf16[512,1024]{1,0:T(8,128)(2,1)S(1)} %copy-done), kind=kOutput, calls=%fused_computation.12 | convolution fusion | flops 543158272 | bytes 9846784 | tf_op jit(solution)/shard_map/qhd,kd->hqk/dot_general | solution.py:30
  23.6 1.7 %fusion.9 = f32[8,512]{1,0:T(8,128)S(1)} fusion(f32[512,512,8]{1,0,2:T(8,128)S(1)} %get-tuple-element.12, f32[8,512]{1,0:T(8,128)S(1)} %get-tuple-element.11, pred[512,512]{0,1:T(8,128)(4,1)S(1)} %get-tuple-element.9), kind=kLoop, calls=%fused_computation.15 | loop fusion | flops 8384512 | bytes 8683520 | tf_op jit(solution)/shard_map/reduce_sum | solution.py:40
  25.4 2.0 %fusion.12 = (f32[8,512]{1,0:T(8,128)S(1)}, f32[512,512,8]{1,0,2:T(8,128)S(1)}) fusion(pred[512,512]{0,1:T(8,128)(4,1)S(1)} %get-tuple-element.10, bf16[512,128]{1,0:T(8,128)(2,1)S(1)} %collective-permute-done.1, bf16[512,1024]{1,0:T(8,128)(2,1)S(1)} %copy-done), kind=kOutput, calls=%fused_computation.21 | convolution fusion | flops 543158272 | bytes 9846784 | tf_op jit(solution)/shard_map/qhd,kd->hqk/dot_general | solution.py:30
  29.2 2.2 %fusion.30 = bf16[512,128]{1,0:T(8,128)(2,1)} fusion(bf16[512,8,128]{0,2,1:T(8,128)(2,1)S(1)} %bitcast.220, f32[512,512,8]{1,0,2:T(8,128)S(1)} %get-tuple-element.14, f32[8,512]{1,0:T(8,128)S(1)} %log_add_fusion, pred[512,512]{0,1:T(8,128)(4,1)S(1)} %get-tuple-element.10), kind=kOutput, calls=%fused_computation.51 | convolution fusion | flops 545325056 | bytes 9846784 | tf_op jit(solution)/shard_map/hqk,qhd->kd/dot_general | solution.py:66
  31.4 2.3 %fusion.31 = bf16[512,128]{1,0:T(8,128)(2,1)} fusion(bf16[512,8,128]{0,2,1:T(8,128)(2,1)S(1)} %bitcast.221, f32[512,512,8]{1,0,2:T(8,128)S(1)} %get-tuple-element.12, f32[8,512]{1,0:T(8,128)S(1)} %log_add_fusion, pred[512,512]{0,1:T(8,128)(4,1)S(1)} %get-tuple-element.9), kind=kOutput, calls=%fused_computation.52 | convolution fusion | flops 545325056 | bytes 9846784 | tf_op jit(solution)/shard_map/hqk,qhd->kd/dot_general | solution.py:66
  33.7 2.3 %convolution_bitcast_fusion.2 = f32[512,128]{1,0:T(8,128)} fusion(bf16[512,8,128]{0,2,1:T(8,128)(2,1)S(1)} %bitcast.222, f32[512,512,8]{1,0,2:T(8,128)S(1)} %get-tuple-element.16, f32[8,512]{1,0:T(8,128)S(1)} %log_add_fusion, pred[512,512]{0,1:T(8,128)(4,1)S(1)} %get-tuple-element.8), kind=kOutput, calls=%fused_computation.44 | convolution fusion | flops 545259520 | bytes 9977856 | tf_op jit(solution)/shard_map/hqk,qhd->kd/dot_general | solution.py:66
  36.0 2.0 %fusion.55 = f32[8,512,128]{1,2,0:T(8,128)S(1)} fusion(bf16[512,128]{1,0:T(8,128)(2,1)S(1)} %copy-done.7, f32[512,512,8]{1,0,2:T(8,128)S(1)} %get-tuple-element.16, f32[8,512]{1,0:T(8,128)S(1)} %log_add_fusion, pred[512,512]{0,1:T(8,128)(4,1)S(1)} %get-tuple-element.8), kind=kOutput, calls=%fused_computation.81 | convolution fusion | flops 545259520 | bytes 10895360 | tf_op jit(solution)/shard_map/hqk,kd->qhd/dot_general | solution.py:53
  37.9 5.8 %collective-permute-start.9 = (bf16[512,128]{1,0:T(8,128)(2,1)}, bf16[512,128]{1,0:T(8,128)(2,1)}, u32[]{:S(2)}, u32[]{:S(2)}) collective-permute-start(bf16[512,128]{1,0:T(8,128)(2,1)} %fusion.31), channel_id=1, source_target_pairs={{8,0},{12,4},{16,8},{20,12},{24,16},{28,20},{9,1},{13,5},{17,9},{2... | collective-permute-start | bytes 393224 | tf_op jit(solution)/shard_map/ppermute | solution.py:17
  43.8 3.9 %collective-permute-start.8 = (bf16[512,128]{1,0:T(8,128)(2,1)}, bf16[512,128]{1,0:T(8,128)(2,1)}, u32[]{:S(2)}, u32[]{:S(2)}) collective-permute-start(bf16[512,128]{1,0:T(8,128)(2,1)} %fusion.30), channel_id=1, source_target_pairs={{4,0},{8,4},{12,8},{16,12},{20,16},{24,20},{28,24},{5,1},{9,5},{13... | collective-permute-start | bytes 393224 | tf_op jit(solution)/shard_map/ppermute | solution.py:17
  47.7 3.3 %fusion.52 = f32[8,512,128]{1,2,0:T(8,128)} fusion(bf16[512,128]{0,1:T(8,128)(2,1)S(1)} %collective-permute-done.4, f32[512,512,8]{1,0,2:T(8,128)S(1)} %get-tuple-element.14, f32[8,512]{1,0:T(8,128)S(1)} %log_add_fusion, pred[512,512]{0,1:T(8,128)(4,1)S(1)} %get-tuple-element.10), kind=kOutput, calls=%fused_computation.78 | convolution fusion | flops 545259520 | bytes 10895360 | tf_op jit(solution)/shard_map/hqk,kd->qhd/dot_general | solution.py:53
  51.0 3.8 %multiply_reduce_fusion = (f32[512,8]{0,1:T(8,128)S(1)}, bf16[8,512,128]{1,2,0:T(8,128)(2,1)S(1)}) fusion(bf16[512,1024]{0,1:T(8,128)(2,1)S(1)} %copy.18, f32[512,512,8]{1,0,2:T(8,128)S(1)} %get-tuple-element.12, f32[8,512]{1,0:T(8,128)S(1)} %log_add_fusion, pred[512,512]{0,1:T(8,128)(4,1)S(1)} %get-tuple-element.9, ...), kind=kOutput, calls=%fused_computation.40 | convolution fusion | flops 548925440 | bytes 15106048 | tf_op jit(solution)/shard_map/hqk,kd->qhd/dot_general | solution.py:53
  54.8 4.2 %fusion.5 = bf16[8,512,512]{1,2,0:T(8,128)(2,1)} fusion(f32[512,512,8]{1,0,2:T(8,128)S(1)} %get-tuple-element.16, f32[8,512]{1,0:T(8,128)S(1)} %bitcast.228, f32[8,512]{1,0:T(8,128)S(1)} %log_add_fusion, pred[512,512]{0,1:T(8,128)(4,1)S(1)} %copy-done.4, bf16[512,8,128]{0,2,1:T(8,128)(2,1)S(1)} %bitcast.223, bf16[512,128]{1,0:T(8,128)(2,1)S(1)} %copy-done.7), kind=kOutput, calls=%fused_computation.8 | convolution fusion | flops 549453824 | bytes 14057472 | tf_op jit(solution)/shard_map/qhd,kd->hqk/dot_general | solution.py:58
  59.0 3.8 %fusion.1 = bf16[8,512,512]{1,2,0:T(8,128)(2,1)S(1)} fusion(f32[512,512,8]{1,0,2:T(8,128)S(1)} %get-tuple-element.12, f32[8,512]{1,0:T(8,128)S(1)} %bitcast.229, f32[8,512]{1,0:T(8,128)S(1)} %log_add_fusion, pred[512,512]{0,1:T(8,128)(4,1)S(1)} %get-tuple-element.9, bf16[512,8,128]{0,2,1:T(8,128)(2,1)S(1)} %bitcast.224, ...), kind=kOutput, calls=%fused_computation.2 | convolution fusion | flops 549453824 | bytes 14057472 | tf_op jit(solution)/shard_map/qhd,kd->hqk/dot_general | solution.py:58
  62.8 1.9 %fusion.32 = bf16[512,128]{1,0:T(8,128)(2,1)} fusion(bf16[8,512,512]{1,2,0:T(8,128)(2,1)S(1)} %fusion.1, bf16[512,1024]{1,0:T(8,128)(2,1)S(1)} %copy-done), kind=kOutput, calls=%fused_computation.53 | convolution fusion | flops 537001984 | bytes 5373952 | tf_op jit(solution)/shard_map/hqk,qhd->kd/dot_general | solution.py:64
  64.7 4.0 %fusion.3 = bf16[8,512,512]{1,2,0:T(8,128)(2,1)S(1)} fusion(f32[512,512,8]{1,0,2:T(8,128)S(1)} %get-tuple-element.14, f32[8,512]{1,0:T(8,128)S(1)} %bitcast.230, f32[8,512]{1,0:T(8,128)S(1)} %log_add_fusion, pred[512,512]{0,1:T(8,128)(4,1)} %copy-done.2, bf16[512,8,128]{0,2,1:T(8,128)(2,1)S(1)} %bitcast.225, bf16[512,128]{0,1:T(8,128)(2,1)} %copy-done.8), kind=kOutput, calls=%fused_computation.5 | convolution fusion | flops 549453824 | bytes 14057472 | tf_op jit(solution)/shard_map/qhd,kd->hqk/dot_general | solution.py:58
  68.7 1.9 %fusion.33 = bf16[512,128]{1,0:T(8,128)(2,1)} fusion(bf16[8,512,512]{1,2,0:T(8,128)(2,1)S(1)} %fusion.3, bf16[512,1024]{1,0:T(8,128)(2,1)S(1)} %copy-done), kind=kOutput, calls=%fused_computation.54 | convolution fusion | flops 537001984 | bytes 5373952 | tf_op jit(solution)/shard_map/hqk,qhd->kd/dot_general | solution.py:64
  70.6 3.9 %collective-permute-start.6 = (bf16[512,128]{1,0:T(8,128)(2,1)}, bf16[512,128]{1,0:T(8,128)(2,1)}, u32[]{:S(2)}, u32[]{:S(2)}) collective-permute-start(bf16[512,128]{1,0:T(8,128)(2,1)} %fusion.33), channel_id=1, source_target_pairs={{4,0},{8,4},{12,8},{16,12},{20,16},{24,20},{28,24},{5,1},{9,5},{13... | collective-permute-start | bytes 393224 | tf_op jit(solution)/shard_map/ppermute | solution.py:17
  74.5 4.6 %collective-permute-start.7 = (bf16[512,128]{1,0:T(8,128)(2,1)}, bf16[512,128]{1,0:T(8,128)(2,1)}, u32[]{:S(2)}, u32[]{:S(2)}) collective-permute-start(bf16[512,128]{1,0:T(8,128)(2,1)} %fusion.32), channel_id=1, source_target_pairs={{8,0},{12,4},{16,8},{20,12},{24,16},{28,20},{9,1},{13,5},{17,9},{2... | collective-permute-start | bytes 393224 | tf_op jit(solution)/shard_map/ppermute | solution.py:17
  84.6 4.2 %add_convert_fusion.2 = bf16[512,128]{1,0:T(8,128)(2,1)} fusion(bf16[512,128]{1,0:T(8,128)(2,1)} %collective-permute-done.7, bf16[512,128]{1,0:T(8,128)(2,1)} %collective-permute-done.6, bf16[8,512,512]{1,2,0:T(8,128)(2,1)} %fusion.5, bf16[512,1024]{1,0:T(8,128)(2,1)S(1)} %copy-done), kind=kOutput, calls=%fused_computation.74 | convolution fusion | flops 537264128 | bytes 5636096 | tf_op jit(solution)/shard_map/hqk,qhd->kd/dot_general | solution.py:64
  (44 shorter events, 18.2 us)
Async XLA Ops:
  0.6 15.8 %copy-start = (bf16[512,1024]{1,0:T(8,128)(2,1)S(1)}, bf16[512,1024]{1,0:T(8,128)(2,1)}, u32[]{:S(2)}) copy-start(bf16[512,1024]{1,0:T(8,128)(2,1)} %param.5) | copy-start | bytes 3145732
  0.6 12.6 %collective-permute-start.2 = (s32[512]{0:T(512)}, s32[512]{0:T(512)S(1)}, u32[]{:S(2)}, u32[]{:S(2)}) collective-permute-start(s32[512]{0:T(512)} %param.9), channel_id=1, source_target_pairs={{0,8},{4,12},{8,16},{12,20},{16,24},{20,28},{1,9},{5,13},{9,17},{1... | collective-permute-start | bytes 6152 | tf_op jit(solution)/shard_map/ppermute | solution.py:17
  2.1 12.5 %collective-permute-start = (s32[512]{0:T(512)}, s32[512]{0:T(512)S(1)}, u32[]{:S(2)}, u32[]{:S(2)}) collective-permute-start(s32[512]{0:T(512)} %param.9), channel_id=1, source_target_pairs={{0,4},{4,8},{8,12},{12,16},{16,20},{20,24},{24,28},{1,5},{5,9},{9,... | collective-permute-start | bytes 6152 | tf_op jit(solution)/shard_map/ppermute | solution.py:17
  6.5 44.5 %collective-permute-start.5 = (bf16[512,128]{0,1:T(8,128)(2,1)S(1)}, bf16[512,128]{0,1:T(8,128)(2,1)}, u32[]{:S(2)}, u32[]{:S(2)}) collective-permute-start(bf16[512,128]{0,1:T(8,128)(2,1)S(1)} %copy.14), channel_id=1, source_target_pairs={{0,8},{4,12},{8,16},{12,20},{16,24},{20,28},{1,9},{5,13},{9,17},{1... | collective-permute-start | bytes 393224 | tf_op jit(solution)/shard_map/ppermute | solution.py:17
  7.8 39.8 %collective-permute-start.4 = (bf16[512,128]{0,1:T(8,128)(2,1)S(1)}, bf16[512,128]{0,1:T(8,128)(2,1)S(1)}, u32[]{:S(2)}, u32[]{:S(2)}) collective-permute-start(bf16[512,128]{0,1:T(8,128)(2,1)S(1)} %copy.14), channel_id=1, source_target_pairs={{0,4},{4,8},{8,12},{12,16},{16,20},{20,24},{24,28},{1,5},{5,9},{9,... | collective-permute-start | bytes 393224 | tf_op jit(solution)/shard_map/ppermute | solution.py:17
  9.8 15.6 %collective-permute-start.1 = (bf16[512,128]{1,0:T(8,128)(2,1)}, bf16[512,128]{1,0:T(8,128)(2,1)S(1)}, u32[]{:S(2)}, u32[]{:S(2)}) collective-permute-start(bf16[512,128]{1,0:T(8,128)(2,1)} %param.6), channel_id=1, source_target_pairs={{0,4},{4,8},{8,12},{12,16},{16,20},{20,24},{24,28},{1,5},{5,9},{9,... | collective-permute-start | bytes 393224 | tf_op jit(solution)/shard_map/ppermute | solution.py:17
  13.2 8.5 %collective-permute-start.3 = (bf16[512,128]{1,0:T(8,128)(2,1)}, bf16[512,128]{1,0:T(8,128)(2,1)S(1)}, u32[]{:S(2)}, u32[]{:S(2)}) collective-permute-start(bf16[512,128]{1,0:T(8,128)(2,1)} %param.6), channel_id=1, source_target_pairs={{0,8},{4,12},{8,16},{12,20},{16,24},{20,28},{1,9},{5,13},{9,17},{1... | collective-permute-start | bytes 393224 | tf_op jit(solution)/shard_map/ppermute | solution.py:17
  16.4 19.6 %copy-start.3 = (pred[512,512]{0,1:T(8,128)(4,1)}, pred[512,512]{0,1:T(8,128)(4,1)S(1)}, u32[]{:S(2)}) copy-start(pred[512,512]{0,1:T(8,128)(4,1)S(1)} %get-tuple-element.8) | copy-start | bytes 786436
  16.4 31.2 %copy-start.2 = (pred[512,512]{0,1:T(8,128)(4,1)}, pred[512,512]{0,1:T(8,128)(4,1)S(1)}, u32[]{:S(2)}) copy-start(pred[512,512]{0,1:T(8,128)(4,1)S(1)} %get-tuple-element.10) | copy-start | bytes 786436
  33.7 2.3 %copy-start.7 = (bf16[512,128]{1,0:T(8,128)(2,1)S(1)}, bf16[512,128]{1,0:T(8,128)(2,1)}, u32[]{:S(2)}) copy-start(bf16[512,128]{1,0:T(8,128)(2,1)} %param.7) | copy-start | bytes 393220
  37.9 50.8 %collective-permute-start.9 = (bf16[512,128]{1,0:T(8,128)(2,1)}, bf16[512,128]{1,0:T(8,128)(2,1)}, u32[]{:S(2)}, u32[]{:S(2)}) collective-permute-start(bf16[512,128]{1,0:T(8,128)(2,1)} %fusion.31), channel_id=1, source_target_pairs={{8,0},{12,4},{16,8},{20,12},{24,16},{28,20},{9,1},{13,5},{17,9},{2... | collective-permute-start | bytes 393224 | tf_op jit(solution)/shard_map/ppermute | solution.py:17
  43.8 45.0 %collective-permute-start.8 = (bf16[512,128]{1,0:T(8,128)(2,1)}, bf16[512,128]{1,0:T(8,128)(2,1)}, u32[]{:S(2)}, u32[]{:S(2)}) collective-permute-start(bf16[512,128]{1,0:T(8,128)(2,1)} %fusion.30), channel_id=1, source_target_pairs={{4,0},{8,4},{12,8},{16,12},{20,16},{24,20},{28,24},{5,1},{9,5},{13... | collective-permute-start | bytes 393224 | tf_op jit(solution)/shard_map/ppermute | solution.py:17
  47.7 3.3 %copy-start.8 = (bf16[512,128]{0,1:T(8,128)(2,1)}, bf16[512,128]{0,1:T(8,128)(2,1)S(1)}, u32[]{:S(2)}) copy-start(bf16[512,128]{0,1:T(8,128)(2,1)S(1)} %collective-permute-done.4) | copy-start | bytes 393220
  51.0 3.8 %copy-start.4 = (pred[512,512]{0,1:T(8,128)(4,1)S(1)}, pred[512,512]{0,1:T(8,128)(4,1)}, u32[]{:S(2)}) copy-start(pred[512,512]{0,1:T(8,128)(4,1)} %copy-done.3) | copy-start | bytes 786436
  64.7 14.4 %copy-start.1 = (bf16[8,512,512]{1,2,0:T(8,128)(2,1)S(1)}, bf16[8,512,512]{1,2,0:T(8,128)(2,1)}, u32[]{:S(2)}) copy-start(bf16[8,512,512]{1,2,0:T(8,128)(2,1)} %fusion.5) | copy-start | bytes 12582916
  64.7 14.4 %copy-start.5 = (bf16[512,128]{1,0:T(8,128)(2,1)S(1)}, bf16[512,128]{1,0:T(8,128)(2,1)}, u32[]{:S(2)}) copy-start(bf16[512,128]{1,0:T(8,128)(2,1)} %param.6) | copy-start | bytes 393220
  70.6 14.0 %collective-permute-start.6 = (bf16[512,128]{1,0:T(8,128)(2,1)}, bf16[512,128]{1,0:T(8,128)(2,1)}, u32[]{:S(2)}, u32[]{:S(2)}) collective-permute-start(bf16[512,128]{1,0:T(8,128)(2,1)} %fusion.33), channel_id=1, source_target_pairs={{4,0},{8,4},{12,8},{16,12},{20,16},{24,20},{28,24},{5,1},{9,5},{13... | collective-permute-start | bytes 393224 | tf_op jit(solution)/shard_map/ppermute | solution.py:17
  74.5 10.1 %collective-permute-start.7 = (bf16[512,128]{1,0:T(8,128)(2,1)}, bf16[512,128]{1,0:T(8,128)(2,1)}, u32[]{:S(2)}, u32[]{:S(2)}) collective-permute-start(bf16[512,128]{1,0:T(8,128)(2,1)} %fusion.32), channel_id=1, source_target_pairs={{8,0},{12,4},{16,8},{20,12},{24,16},{28,20},{9,1},{13,5},{17,9},{2... | collective-permute-start | bytes 393224 | tf_op jit(solution)/shard_map/ppermute | solution.py:17
  80.8 8.0 %copy-start.6 = (f32[512,128]{1,0:T(8,128)S(1)}, f32[512,128]{1,0:T(8,128)}, u32[]{:S(2)}) copy-start(f32[512,128]{1,0:T(8,128)} %convolution_bitcast_fusion.2) | copy-start | bytes 786436
where the time goes:
time: 91 us; the launch traced here: 90.5 us
  matrix products  45.1 us (50%)
  starting transfers between devices  29.5 us (32%)
  other arithmetic  8.74 us (10%)
  local copies, waits for them, and re-layouts  5.17 us (6%)
  waiting for transfers between devices  1 us (1%)
  between operations  0.96 us (1%)
    ppermute x10, starting transfers between devices, shifted(): lax.ppermute(value, axis, [(source, source + steps) for source in range(f...  29.5 us
    dot_general x3, matrix products, pair_backward(): jnp.einsum('qhd,kd->hqk', grad_tile, value_tile, preferred_element_type=j...  12 us
    dot_general x3, matrix products, pair_output(): jnp.einsum('hqk,kd->qhd', probs_low, value_tile, preferred_element_type=j...  9.04 us
    dot_general x3, matrix products, pair_backward(): jnp.einsum('hqk,qhd->kd', dscores, query_tile, preferred_element_type=jnp...  8 us
    dot_general x3, matrix products, pair_backward(): jnp.einsum('hqk,qhd->kd', probs_low, grad_tile, preferred_element_type=jn...  6.79 us
    dot_general x3, matrix products, pair_scores(): jnp.einsum('qhd,kd->hqk', query_tile, key_tile, preferred_element_type=jn...  6.48 us
    reduce_sum x3, other arithmetic, pair_stats(): jnp.sum(jnp.where(allowed[None], jnp.exp(scores - peak[..., None]), 0.0),...  5.2 us
    unnamed x22, local copies, waits for them, and re-layouts  5.17 us
  transfers between devices with their start and end apart: 10, of which 1 were waited for; matrix products, arithmetic and copies ran while one was open for 63% of the time, Pallas kernels for 0%

commit v1 on v0

v1 whole, which is shorter than its diff:
```python
import functools
import math

import jax
import jax.numpy as jnp
from jax import lax
from jax.experimental import pallas as pl
from jax.experimental.pallas import tpu as pltpu
from jax.sharding import PartitionSpec as P

REACH = 2
NEG = -1e30
MESH = pl.DeviceIdType.MESH
NT = (((1,), (1,)), ((), ()))
F32 = jnp.float32
BF16 = jnp.bfloat16


def dot(a, b):
    return jnp.dot(a, b, preferred_element_type=F32)


def dot_nt(a, b):
    return lax.dot_general(a, b, NT, preferred_element_type=F32)


def kernel(
    n, heads, rows, size, block,
    k_ref, v_ref, seg_ref, q_hbm, g_hbm,
    o_hbm, dq_hbm, dk_ref, dv_ref,
    q_s, g_s, o_s, dq_s, kwin, vwin, segwin, ktw, vtw, kt0, vt0,
    bias0, biasw, pun, m_s, l_s, acc_s, f_s, delta_s, dqt_s,
    dkw, dvw, dk0, dv0, outbox, inbox,
    in_sem, out_sem, send_sem, recv_sem, bsend_sem, brecv_sem,
):
    me = lax.axis_index("cp")
    scale = 1.0 / math.sqrt(size)
    c2 = scale * math.log2(math.e)
    blocks = rows // block
    far = REACH * rows
    lanes = seg_ref.shape[1]
    chunks = rows // lanes

    def fetch(h):
        cols = pl.ds(pl.multiple_of(h * size, size), size)
        return (
            pltpu.make_async_copy(q_hbm.at[:, cols], q_s.at[h], in_sem.at[0, h]),
            pltpu.make_async_copy(g_hbm.at[:, cols], g_s.at[h], in_sem.at[1, h]),
        )

    def put(h):
        cols = pl.ds(pl.multiple_of(h * size, size), size)
        return (
            pltpu.make_async_copy(o_s.at[h], o_hbm.at[:, cols], out_sem.at[0, h]),
            pltpu.make_async_copy(dq_s.at[h], dq_hbm.at[:, cols], out_sem.at[1, h]),
        )

    @pl.loop(0, heads)
    def _(h):
        for copy in fetch(h):
            copy.start()

    barrier = pltpu.get_barrier_semaphore()
    steps = (-2, -1, 1, 2)

    def there(step):
        return me + step >= 0 if step < 0 else me + step < n

    for step in steps:

        @pl.when(there(step))
        def _():
            pl.semaphore_signal(barrier, inc=1, device_id={"cp": me + step}, device_id_type=MESH)

    pl.semaphore_wait(barrier, jnp.minimum(me, REACH) + jnp.minimum(n - 1 - me, REACH))

    def forward(dist):
        at = pl.ds((REACH - dist) * rows, rows)
        pairs = (
            (seg_ref, segwin.at[REACH - dist]),
            (k_ref, kwin.at[at]),
            (v_ref, vwin.at[at]),
        )
        return [
            pltpu.make_async_remote_copy(
                src_ref=src, dst_ref=dst,
                send_sem=send_sem.at[i, dist - 1], recv_sem=recv_sem.at[i, dist - 1],
                device_id={"cp": me + dist}, device_id_type=MESH,
            )
            for i, (src, dst) in enumerate(pairs)
        ]

    def back(dist):
        return [
            pltpu.make_async_remote_copy(
                src_ref=outbox.at[i, dist - 1], dst_ref=inbox.at[i, dist - 1],
                send_sem=bsend_sem.at[i, dist - 1], recv_sem=brecv_sem.at[i, dist - 1],
                device_id={"cp": me - dist}, device_id_type=MESH,
            )
            for i in range(2)
        ]

    for dist in (1, 2):

        @pl.when(there(dist))
        def _():
            for copy in forward(dist):
                copy.start()

    seg_own = seg_ref[...].astype(F32)
    line = lax.broadcasted_iota(jnp.int32, (lanes, lanes), 0)
    lane = lax.broadcasted_iota(jnp.int32, (lanes, lanes), 1)
    for kc in range(chunks):
        col = jnp.transpose(jnp.broadcast_to(seg_own[kc : kc + 1], (lanes, lanes)))
        for qc in range(chunks):
            same = col == seg_own[qc : qc + 1]
            if kc == qc:
                same = same & (line <= lane)
            value = jnp.where(same, 0.0, NEG) if kc <= qc else jnp.full((lanes, lanes), NEG, F32)
            bias0[kc * lanes : (kc + 1) * lanes, qc * lanes : (qc + 1) * lanes] = value
    kt0[...] = jnp.transpose(k_ref[...])
    vt0[...] = jnp.transpose(v_ref[...])
    dkw[...] = jnp.zeros_like(dkw)
    dvw[...] = jnp.zeros_like(dvw)
    dk0[...] = jnp.zeros_like(dk0)
    dv0[...] = jnp.zeros_like(dv0)

    @pl.loop(0, heads)
    def _(h):
        for copy in fetch(h):
            copy.wait()
        for b in range(blocks):
            qs = slice(b * block, (b + 1) * block)
            ks = slice(0, (b + 1) * block)
            s = dot_nt(k_ref[ks], q_s[h, qs]) * c2 + bias0[ks, qs]
            m = jnp.max(s, axis=0, keepdims=True)
            p = jnp.exp2(s - m)
            low = p.astype(BF16)
            pun[h, ks, qs] = low
            m_s[h, :, qs] = m
            l_s[h, :, qs] = jnp.sum(p, axis=0, keepdims=True)
            acc_s[h, :, qs] = dot(vt0[:, ks], low)

    for dist in (1, 2):
        at = slice((REACH - dist) * rows, (REACH - dist + 1) * rows)

        @pl.when(there(-dist))
        def _():
            for copy in forward(dist):
                copy.wait_recv()

        @pl.when(me - dist < 0)
        def _():
            kwin[at] = jnp.zeros((rows, size), BF16)
            vwin[at] = jnp.zeros((rows, size), BF16)
            segwin[REACH - dist] = jnp.full((chunks, lanes), -1, jnp.int32)

    for slot in range(REACH):
        seg_far = segwin[slot].astype(F32)
        at = slice(slot * rows, (slot + 1) * rows)
        for kc in range(chunks):
            col = jnp.transpose(jnp.broadcast_to(seg_far[kc : kc + 1], (lanes, lanes)))
            top = slot * rows + kc * lanes
            for qc in range(chunks):
                value = jnp.where(col == seg_own[qc : qc + 1], 0.0, NEG)
                biasw[top : top + lanes, qc * lanes : (qc + 1) * lanes] = value
        ktw[:, at] = jnp.transpose(kwin[at])
        vtw[:, at] = jnp.transpose(vwin[at])

    def far_start(b):
        return b * block

    @pl.loop(0, heads)
    def _(h):
        for b in range(blocks):
            qs = slice(b * block, (b + 1) * block)
            ks = slice(far_start(b), far)
            qb = q_s[h, qs]
            gb = g_s[h, qs]
            s = dot_nt(kwin[ks], qb) * c2 + biasw[ks, qs]
            m0 = m_s[h, :, qs]
            m = jnp.maximum(m0, jnp.max(s, axis=0, keepdims=True))
            p = jnp.exp2(s - m)
            a = jnp.exp2(m0 - m)
            inv = 1.0 / (l_s[h, :, qs] * a + jnp.sum(p, axis=0, keepdims=True))
            f0 = a * inv
            p = p * inv
            low = p.astype(BF16)
            out = (acc_s[h, :, qs] * f0 + dot(vtw[:, ks], low)).astype(BF16)
            gt = jnp.transpose(gb.astype(F32))
            outf = out.astype(F32)
            delta = jnp.sum(gt * outf, axis=0, keepdims=True)
            o_s[h, qs] = jnp.transpose(outf).astype(BF16)
            dp = dot_nt(vwin[ks], gb)
            ds = (p * (dp - delta)).astype(BF16)
            dqt_s[h, :, qs] = dot(ktw[:, ks], ds)
            dvw[ks] += dot(low, gb)
            dkw[ks] += dot(ds, qb)
            f_s[h, :, qs] = f0
            delta_s[h, :, qs] = delta
        put(h)[0].start()

    for dist in (1, 2):
        at = slice((REACH - dist) * rows, (REACH - dist + 1) * rows)
        outbox[0, dist - 1] = (dkw[at] * scale).astype(BF16)
        outbox[1, dist - 1] = dvw[at].astype(BF16)

    for dist in (1, 2):

        @pl.when(there(-dist))
        def _():
            for copy in back(dist):
                copy.start()

    @pl.loop(0, heads)
    def _(h):
        for b in range(blocks):
            qs = slice(b * block, (b + 1) * block)
            ks = slice(0, (b + 1) * block)
            qb = q_s[h, qs]
            gb = g_s[h, qs]
            p = pun[h, ks, qs].astype(F32) * f_s[h, :, qs]
            low = p.astype(BF16)
            dp = dot_nt(v_ref[ks], gb)
            ds = (p * (dp - delta_s[h, :, qs])).astype(BF16)
            dqt = dqt_s[h, :, qs] + dot(kt0[:, ks], ds)
            dq_s[h, qs] = jnp.transpose(dqt * scale).astype(BF16)
            dv0[ks] += dot(low, gb)
            dk0[ks] += dot(ds, qb)
        put(h)[1].start()

    dk0[...] = dk0[...] * scale
    for dist in (1, 2):

        @pl.when(there(dist))
        def _():
            for copy in back(dist):
                copy.wait_recv()
            dk0[...] += inbox[0, dist - 1].astype(F32)
            dv0[...] += inbox[1, dist - 1].astype(F32)

    dk_ref[...] = dk0[...].astype(BF16)
    dv_ref[...] = dv0[...].astype(BF16)

    for dist in (1, 2):

        @pl.when(there(dist))
        def _():
            for copy in forward(dist):
                copy.wait_send()

        @pl.when(there(-dist))
        def _():
            for copy in back(dist):
                copy.wait_send()

    @pl.loop(0, heads)
    def _(h):
        for copy in put(h):
            copy.wait()


def on_device(n, queries, keys, values, grad_out, segments):
    rows, width = queries.shape
    size = keys.shape[1]
    heads = width // size
    block = rows // 2
    lanes = 128
    far = REACH * rows
    vmem = pl.BlockSpec(memory_space=pltpu.VMEM)
    hbm = pl.BlockSpec(memory_space=pl.ANY)
    wide = jax.ShapeDtypeStruct((rows, width), BF16)
    thin = jax.ShapeDtypeStruct((rows, size), BF16)
    stack = pltpu.VMEM((heads, rows, size), BF16)
    row = pltpu.VMEM((heads, 1, rows), F32)
    tall = pltpu.VMEM((heads, size, rows), F32)
    dma = pltpu.SemaphoreType.DMA
    return pl.pallas_call(
        functools.partial(kernel, n, heads, rows, size, block),
        out_shape=(wide, wide, thin, thin),
        in_specs=[vmem, vmem, vmem, hbm, hbm],
        out_specs=(hbm, hbm, vmem, vmem),
        scratch_shapes=[
            stack, stack, stack, stack,
            pltpu.VMEM((far, size), BF16), pltpu.VMEM((far, size), BF16),
            pltpu.VMEM((REACH, rows // lanes, lanes), jnp.int32),
            pltpu.VMEM((size, far), BF16), pltpu.VMEM((size, far), BF16),
            pltpu.VMEM((size, rows), BF16), pltpu.VMEM((size, rows), BF16),
            pltpu.VMEM((rows, rows), F32), pltpu.VMEM((far, rows), F32),
            pltpu.VMEM((heads, rows, rows), BF16),
            row, row, tall, row, row, tall,
            pltpu.VMEM((far, size), F32), pltpu.VMEM((far, size), F32),
            pltpu.VMEM((rows, size), F32), pltpu.VMEM((rows, size), F32),
            pltpu.VMEM((2, REACH, rows, size), BF16), pltpu.VMEM((2, REACH, rows, size), BF16),
            dma((2, heads)), dma((2, heads)),
            dma((3, REACH)), dma((3, REACH)), dma((2, REACH)), dma((2, REACH)),
        ],
        compiler_params=pltpu.CompilerParams(
            collective_id=0, has_side_effects=True, vmem_limit_bytes=60 * 1024 * 1024
        ),
    )(keys, values, segments.reshape(rows // lanes, lanes), queries, grad_out)


def solution(mesh):
    placed = (P("cp", "grp"), P("cp", "grp"), P("cp", "grp"), P("cp", "grp"), P("cp"))
    return jax.shard_map(
        functools.partial(on_device, mesh.shape["cp"]),
        mesh=mesh,
        in_specs=placed,
        out_specs=(P("cp", "grp"), P("cp", "grp"), P("cp", "grp"), P("cp", "grp")),
        check_vma=False,
    )
```

time: 91 us -> 54.5 us (0.60)
  the two profiles are of different devices: /device:TPU:26 before, /device:TPU:0 now
where the time goes in v1:
time: 54.5 us; the launch traced here: 54.3 us
  Pallas kernels  48.7 us (89%)
  local copies, waits for them, and re-layouts  4.98 us (9%)
  between operations  0.65 us (1%)
    pallas_call x1, Pallas kernels, on_device(): pl.pallas_call(functools.partial(kernel, n, heads, rows, size, block), ou...  48.7 us
    unnamed x10, local copies, waits for them, and re-layouts  4.98 us

profile of v1, /device:TPU:0, one launch (start us, length us, event | category | flops | bytes accessed | tf_op | source)
XLA Modules:
  0.0 54.3 jit_solution(3977295103893594627)
XLA Ops:
  0.6 48.7 %shard_map.84 = (bf16[512,1024]{1,0:T(8,128)(2,1)}, bf16[512,1024]{1,0:T(8,128)(2,1)}, bf16[512,128]{1,0:T(8,128)(2,1)}, bf16[512,128]{1,0:T(8,128)(2,1)}) custom-call(bf16[512,128]{1,0:T(8,128)(2,1)} %k_ref.1, bf16[512,128]{1,0:T(8,128)(2,1)} %v_ref.1, s32[4,128]{1,0:T(4,128)} %bitcast.1, bf16[512,1024]{1,0:T(8,128)(2,1)} %q_hbm.1, bf16[512,1024]{1,0:T(8,128)(2,1)} %g_hbm.1), custom_call_target="tpu_custom_call" | custom-call | tf_op jit(solution)/shard_map/pallas_call | solution.py:278
  49.3 0.0 copy-start
  49.3 2.4 %copy.13 = bf16[512,1024]{1,0:T(8,128)(2,1)} copy(bf16[512,1024]{1,0:T(8,128)(2,1)} %get-tuple-element.8) | data formatting | bytes 2097152
  51.7 0.0 copy-done
  51.7 0.0 copy-start.2
  51.7 1.0 %copy.14 = bf16[512,1024]{1,0:T(8,128)(2,1)} copy(bf16[512,1024]{1,0:T(8,128)(2,1)S(1)} %copy-done) | data formatting | bytes 2097152
  52.7 0.1 copy-done.2
  52.7 0.0 copy-start.1
  52.7 0.7 %copy.15 = bf16[512,128]{1,0:T(8,128)(2,1)} copy(bf16[512,128]{1,0:T(8,128)(2,1)S(1)} %copy-done.2) | data formatting | bytes 262144
  53.4 0.3 copy-done.1
  53.7 0.7 %copy.16 = bf16[512,128]{1,0:T(8,128)(2,1)} copy(bf16[512,128]{1,0:T(8,128)(2,1)S(1)} %copy-done.1) | data formatting | bytes 262144
Async XLA Ops:
  49.3 2.4 %copy-start = (bf16[512,1024]{1,0:T(8,128)(2,1)S(1)}, bf16[512,1024]{1,0:T(8,128)(2,1)}, u32[]{:S(2)}) copy-start(bf16[512,1024]{1,0:T(8,128)(2,1)} %get-tuple-element.9) | copy-start | bytes 3145732
  51.7 1.0 %copy-start.2 = (bf16[512,128]{1,0:T(8,128)(2,1)S(1)}, bf16[512,128]{1,0:T(8,128)(2,1)}, u32[]{:S(2)}) copy-start(bf16[512,128]{1,0:T(8,128)(2,1)} %get-tuple-element.10) | copy-start | bytes 393220
  52.7 1.0 %copy-start.1 = (bf16[512,128]{1,0:T(8,128)(2,1)S(1)}, bf16[512,128]{1,0:T(8,128)(2,1)}, u32[]{:S(2)}) copy-start(bf16[512,128]{1,0:T(8,128)(2,1)} %get-tuple-element.11) | copy-start | bytes 393220

commit v2 on v1

--- a/solution.py
+++ b/solution.py
@@ -30,7 +30,7 @@
     o_hbm, dq_hbm, dk_ref, dv_ref,
     q_s, g_s, o_s, dq_s, kwin, vwin, segwin, ktw, vtw, kt0, vt0,
     bias0, biasw, pun, m_s, l_s, acc_s, f_s, delta_s, dqt_s,
-    dkw, dvw, dk0, dv0, outbox, inbox,
+    dkw, dvw, dk0, dv0, outbox, inbox, s_s, low_s, ds_s,
     in_sem, out_sem, send_sem, recv_sem, bsend_sem, brecv_sem,
 ):
     me = lax.axis_index("cp")
@@ -38,6 +38,7 @@
     c2 = scale * math.log2(math.e)
     blocks = rows // block
     far = REACH * rows
+    cut = block // 1
     lanes = seg_ref.shape[1]
     chunks = rows // lanes
 
@@ -125,21 +126,60 @@
     dk0[...] = jnp.zeros_like(dk0)
     dv0[...] = jnp.zeros_like(dv0)
 
+    def local_chunks():
+        return [(k, k + cut, k // block * block, rows) for k in range(0, rows, cut)]
+
+    def far_chunks():
+        return [(k, k + cut, 0, min(rows, (k // block + 1) * block)) for k in range(0, far, cut)]
+
+    def eights(x):
+        return x.reshape(x.shape[0] // 8, 8, x.shape[1])
+
+    def scores(h, chunks_of, keys, bias, tops):
+        for k0, k1, q0, q1 in chunks_of:
+            s = dot_nt(keys[k0:k1], q_s[h, q0:q1]) * c2 + bias[k0:k1, q0:q1]
+            s_s[k0:k1, q0:q1] = s
+            top = jnp.max(eights(s), axis=0)
+            for b in range(q0 // block, q1 // block):
+                part = top[:, b * block - q0 : (b + 1) * block - q0]
+                tops[b] = part if tops[b] is None else jnp.maximum(tops[b], part)
+        return jnp.concatenate([jnp.max(t, axis=0, keepdims=True) for t in tops], axis=1)
+
+    def weights(chunks_of, m, store):
+        sums = [None] * blocks
+        for k0, k1, q0, q1 in chunks_of:
+            p = jnp.exp2(s_s[k0:k1, q0:q1] - m[:, q0:q1])
+            store[k0:k1, q0:q1] = p.astype(BF16)
+            part = jnp.sum(eights(p), axis=0)
+            for b in range(q0 // block, q1 // block):
+                one = part[:, b * block - q0 : (b + 1) * block - q0]
+                sums[b] = one if sums[b] is None else sums[b] + one
+        return jnp.concatenate([jnp.sum(t, axis=0, keepdims=True) for t in sums], axis=1)
+
+    def back_chunks(h, chunks_of, low_of, factor, delta, values, dk_sum, dv_sum):
+        for k0, k1, q0, q1 in chunks_of:
+            p = low_of[k0:k1, q0:q1].astype(F32) * factor[:, q0:q1]
+            dp = dot_nt(values[k0:k1], g_s[h, q0:q1])
+            ds = (p * (dp - delta[:, q0:q1])).astype(BF16)
+            ds_s[k0:k1, q0:q1] = ds
+            dv_sum[k0:k1] += dot(p.astype(BF16), g_s[h, q0:q1])
+            dk_sum[k0:k1] += dot(ds, q_s[h, q0:q1])
+
+    def local_dot(left, right):
+        return [dot(left[:, : (b + 1) * block], right[: (b + 1) * block, b * block : (b + 1) * block]) for b in range(blocks)]
+
+    def far_dot(left, right):
+        return [dot(left[:, b * block :], right[b * block :, b * block : (b + 1) * block]) for b in range(blocks)]
+
     @pl.loop(0, heads)
     def _(h):
         for copy in fetch(h):
             copy.wait()
-        for b in range(blocks):
-            qs = slice(b * block, (b + 1) * block)
-            ks = slice(0, (b + 1) * block)
-            s = dot_nt(k_ref[ks], q_s[h, qs]) * c2 + bias0[ks, qs]
-            m = jnp.max(s, axis=0, keepdims=True)
-            p = jnp.exp2(s - m)
-            low = p.astype(BF16)
-            pun[h, ks, qs] = low
-            m_s[h, :, qs] = m
-            l_s[h, :, qs] = jnp.sum(p, axis=0, keepdims=True)
-            acc_s[h, :, qs] = dot(vt0[:, ks], low)
+        m = scores(h, local_chunks(), k_ref, bias0, [None] * blocks)
+        m_s[h] = m
+        l_s[h] = weights(local_chunks(), m, pun.at[h])
+        for b, part in enumerate(local_dot(vt0, pun.at[h])):
+            acc_s[h, :, b * block : (b + 1) * block] = part
 
     for dist in (1, 2):
         at = slice((REACH - dist) * rows, (REACH - dist + 1) * rows)
@@ -167,37 +207,26 @@
         ktw[:, at] = jnp.transpose(kwin[at])
         vtw[:, at] = jnp.transpose(vwin[at])
 
-    def far_start(b):
-        return b * block
-
-    @pl.loop(0, heads)
-    def _(h):
-        for b in range(blocks):
+    @pl.loop(0, heads)
+    def _(h):
+        m0 = m_s[h]
+        m = jnp.maximum(m0, scores(h, far_chunks(), kwin, biasw, [None] * blocks))
+        a = jnp.exp2(m0 - m)
+        inv = 1.0 / (l_s[h] * a + weights(far_chunks(), m, low_s))
+        f0 = a * inv
+        f_s[h] = f0
+        deltas = []
+        for b, part in enumerate(far_dot(vtw, low_s)):
             qs = slice(b * block, (b + 1) * block)
-            ks = slice(far_start(b), far)
-            qb = q_s[h, qs]
-            gb = g_s[h, qs]
-            s = dot_nt(kwin[ks], qb) * c2 + biasw[ks, qs]
-            m0 = m_s[h, :, qs]
-            m = jnp.maximum(m0, jnp.max(s, axis=0, keepdims=True))
-            p = jnp.exp2(s - m)
-            a = jnp.exp2(m0 - m)
-            inv = 1.0 / (l_s[h, :, qs] * a + jnp.sum(p, axis=0, keepdims=True))
-            f0 = a * inv
-            p = p * inv
-            low = p.astype(BF16)
-            out = (acc_s[h, :, qs] * f0 + dot(vtw[:, ks], low)).astype(BF16)
-            gt = jnp.transpose(gb.astype(F32))
-            outf = out.astype(F32)
-            delta = jnp.sum(gt * outf, axis=0, keepdims=True)
-            o_s[h, qs] = jnp.transpose(outf).astype(BF16)
-            dp = dot_nt(vwin[ks], gb)
-            ds = (p * (dp - delta)).astype(BF16)
-            dqt_s[h, :, qs] = dot(ktw[:, ks], ds)
-            dvw[ks] += dot(low, gb)
-            dkw[ks] += dot(ds, qb)
-            f_s[h, :, qs] = f0
-            delta_s[h, :, qs] = delta
+            out = (acc_s[h, :, qs] * f0[:, qs] + part * inv[:, qs]).astype(BF16).astype(F32)
+            gt = jnp.transpose(g_s[h, qs].astype(F32))
+            deltas.append(jnp.sum(gt * out, axis=0, keepdims=True))
+            o_s[h, qs] = jnp.transpose(out).astype(BF16)
+        delta = jnp.concatenate(deltas, axis=1)
+        delta_s[h] = delta
+        back_chunks(h, far_chunks(), low_s, inv, delta, vwin, dkw, dvw)
+        for b, part in enumerate(far_dot(ktw, ds_s)):
+            dqt_s[h, :, b * block : (b + 1) * block] = part
         put(h)[0].start()
 
     for dist in (1, 2):
@@ -214,19 +243,10 @@
 
     @pl.loop(0, heads)
     def _(h):
-        for b in range(blocks):
+        back_chunks(h, local_chunks(), pun.at[h], f_s[h], delta_s[h], v_ref, dk0, dv0)
+        for b, part in enumerate(local_dot(kt0, ds_s)):
             qs = slice(b * block, (b + 1) * block)
-            ks = slice(0, (b + 1) * block)
-            qb = q_s[h, qs]
-            gb = g_s[h, qs]
-            p = pun[h, ks, qs].astype(F32) * f_s[h, :, qs]
-            low = p.astype(BF16)
-            dp = dot_nt(v_ref[ks], gb)
-            ds = (p * (dp - delta_s[h, :, qs])).astype(BF16)
-            dqt = dqt_s[h, :, qs] + dot(kt0[:, ks], ds)
-            dq_s[h, qs] = jnp.transpose(dqt * scale).astype(BF16)
-            dv0[ks] += dot(low, gb)
-            dk0[ks] += dot(ds, qb)
+            dq_s[h, qs] = jnp.transpose((dqt_s[h, :, qs] + part) * scale).astype(BF16)
         put(h)[1].start()
 
     dk0[...] = dk0[...] * scale
@@ -292,6 +312,7 @@
             pltpu.VMEM((far, size), F32), pltpu.VMEM((far, size), F32),
             pltpu.VMEM((rows, size), F32), pltpu.VMEM((rows, size), F32),
             pltpu.VMEM((2, REACH, rows, size), BF16), pltpu.VMEM((2, REACH, rows, size), BF16),
+            pltpu.VMEM((far, rows), F32), pltpu.VMEM((far, rows), BF16), pltpu.VMEM((far, rows), BF16),
             dma((2, heads)), dma((2, heads)),
             dma((3, REACH)), dma((3, REACH)), dma((2, REACH)), dma((2, REACH)),
         ],

time: 54.5 us -> 46.5 us (0.85)
  Pallas kernels: 48.7 us -> 40.7 us
    pallas_call x1, Pallas kernels: 48.7 us -> 40.7 us  [on_device(): pl.pallas_call(functools.partial(kernel, n, heads, rows, size, block), ou...]
where the time goes in v2:
time: 46.5 us; the launch traced here: 46.3 us
  Pallas kernels  40.7 us (88%)
  local copies, waits for them, and re-layouts  4.98 us (11%)
  between operations  0.65 us (1%)
    pallas_call x1, Pallas kernels, on_device(): pl.pallas_call(functools.partial(kernel, n, heads, rows, size, block), ou...  40.7 us
    unnamed x10, local copies, waits for them, and re-layouts  4.98 us

profile of v2, /device:TPU:0, one launch (start us, length us, event | category | flops | bytes accessed | tf_op | source)
XLA Modules:
  0.0 46.3 jit_solution(9500631973410111701)
XLA Ops:
  0.6 40.7 %shard_map.84 = (bf16[512,1024]{1,0:T(8,128)(2,1)}, bf16[512,1024]{1,0:T(8,128)(2,1)}, bf16[512,128]{1,0:T(8,128)(2,1)}, bf16[512,128]{1,0:T(8,128)(2,1)}) custom-call(bf16[512,128]{1,0:T(8,128)(2,1)} %k_ref.1, bf16[512,128]{1,0:T(8,128)(2,1)} %v_ref.1, s32[4,128]{1,0:T(4,128)} %bitcast.1, bf16[512,1024]{1,0:T(8,128)(2,1)} %q_hbm.1, bf16[512,1024]{1,0:T(8,128)(2,1)} %g_hbm.1), custom_call_target="tpu_custom_call" | custom-call | tf_op jit(solution)/shard_map/pallas_call | solution.py:298
  41.3 0.0 copy-start
  41.3 2.4 %copy.13 = bf16[512,1024]{1,0:T(8,128)(2,1)} copy(bf16[512,1024]{1,0:T(8,128)(2,1)} %get-tuple-element.8) | data formatting | bytes 2097152
  43.7 0.0 copy-done
  43.7 0.0 copy-start.2
  43.7 1.0 %copy.14 = bf16[512,1024]{1,0:T(8,128)(2,1)} copy(bf16[512,1024]{1,0:T(8,128)(2,1)S(1)} %copy-done) | data formatting | bytes 2097152
  44.7 0.1 copy-done.2
  44.7 0.0 copy-start.1
  44.7 0.7 %copy.15 = bf16[512,128]{1,0:T(8,128)(2,1)} copy(bf16[512,128]{1,0:T(8,128)(2,1)S(1)} %copy-done.2) | data formatting | bytes 262144
  45.4 0.3 copy-done.1
  45.7 0.7 %copy.16 = bf16[512,128]{1,0:T(8,128)(2,1)} copy(bf16[512,128]{1,0:T(8,128)(2,1)S(1)} %copy-done.1) | data formatting | bytes 262144
Async XLA Ops:
  41.3 2.4 %copy-start = (bf16[512,1024]{1,0:T(8,128)(2,1)S(1)}, bf16[512,1024]{1,0:T(8,128)(2,1)}, u32[]{:S(2)}) copy-start(bf16[512,1024]{1,0:T(8,128)(2,1)} %get-tuple-element.9) | copy-start | bytes 3145732
  43.7 1.0 %copy-start.2 = (bf16[512,128]{1,0:T(8,128)(2,1)S(1)}, bf16[512,128]{1,0:T(8,128)(2,1)}, u32[]{:S(2)}) copy-start(bf16[512,128]{1,0:T(8,128)(2,1)} %get-tuple-element.10) | copy-start | bytes 393220
  44.7 1.0 %copy-start.1 = (bf16[512,128]{1,0:T(8,128)(2,1)S(1)}, bf16[512,128]{1,0:T(8,128)(2,1)}, u32[]{:S(2)}) copy-start(bf16[512,128]{1,0:T(8,128)(2,1)} %get-tuple-element.11) | copy-start | bytes 393220
